TPU v7x, 32 devices: a whole 2x2x4 slice. The times are simulated.
32 devices in a mesh: acct: 8 (over z, y), rep: 4 (over x, core).
Axes of the slice: x: 2, y: 2, z: 4, core: 2. Of those that a mesh axis runs over, the one named last changes fastest.
Arguments:
- memory: bfloat16 [262144, 256], P(('acct', 'rep')), may hold values from -4 to 4
- features: bfloat16 [4096, 128], P(('acct', 'rep')), may hold values from -6 to 6
- buckets: int32 [4096], P(('acct', 'rep')), may hold values from 0 to 4095
- src_owner: int32 [4096, 1], P(('acct', 'rep')), may hold values from 0 to 31; in each aligned block of 128 rows (0 to 127, 128 to 255, ...) at most 8 rows name the same one
- src_slot: int32 [4096], P(('acct', 'rep')), may hold values from 0 to 8191
- dst_owner: int32 [4096, 1], P(('acct', 'rep')), may hold values from 0 to 31; in each aligned block of 128 rows (0 to 127, 128 to 255, ...) at most 8 rows name the same one
- dst_slot: int32 [4096], P(('acct', 'rep')), may hold values from 0 to 8191
- nb_owner: int32 [4096, 10, 1], P(('acct', 'rep')), may hold values from 0 to 31; in each aligned block of 1280 rows (0 to 1279, 1280 to 2559, ..., all dimensions but the last counted through in order) at most 80 rows name the same one
- nb_slot: int32 [4096, 10], P(('acct', 'rep')), may hold values from 0 to 8191
- w_msg: bfloat16 [512, 128], replicated, may hold values from -0.25 to 0.25
- w_in: bfloat16 [128, 768], replicated, may hold values from -0.5 to 0.5
- u_zr: bfloat16 [256, 512], replicated, may hold values from -0.375 to 0.375
- u_h: bfloat16 [256, 256], replicated, may hold values from -0.375 to 0.375
- w_query: bfloat16 [256, 256], replicated, may hold values from -0.375 to 0.375
- w_key: bfloat16 [256, 256], replicated, may hold values from -0.375 to 0.375
- w_value: bfloat16 [256, 256], replicated, may hold values from -0.375 to 0.375
- emb_grad: bfloat16 [4096, 256], P(('acct', 'rep')), may hold values from -6 to 6
Outputs:
- new_memory: bfloat16 [262144, 256], P(('acct', 'rep'))
- embedding: bfloat16 [4096, 256], P(('acct', 'rep'))
- grad_msg: float32 [512, 128], replicated
- grad_in: float32 [128, 768], replicated
- grad_zr: float32 [256, 512], replicated
- grad_h: float32 [256, 256], replicated
- grad_query: float32 [256, 256], replicated
- grad_key: float32 [256, 256], replicated
- grad_value: float32 [256, 256], replicated
Inputs may be any that keep to these rules, and one draw needn't show every extreme that they name: `src_owner`: in each aligned block of 128 events (one device's events) at most 8 events name one owner, a bound that some block reaches. `dst_owner`: in each aligned block of 128 events at most 8 events name one owner, a bound that some block reaches. `nb_owner`: in each aligned block of 128 events (1280 entries) at most 80 entries name one owner, a bound that some block reaches.
All inputs are finite; a program needn't handle non-finite values.
Results may differ from a plain program's by a relative error of at most 0.01.
Values may be sent and summed in bfloat16 or wider, within the bound.
No kernel may reach another device: no remote copies, remote signals or barrier semaphores. Data moves between devices by JAX's collectives and lax.ppermute only.
A program may use at most 192 MiB of HBM per device.

v0:
```python
import math
import jax
import jax.numpy as jnp
from jax import lax
from jax.sharding import PartitionSpec as P

HEADS = 2
cap_value = 10.0


def widen(tensor):
    return lax.optimization_barrier(tensor).astype(jnp.float32)


def time_code(buckets, code_width):
    column = jnp.arange(code_width, dtype=jnp.float32)
    frequency = jnp.exp(column * (-11.5 / code_width))
    return jnp.cos(buckets.astype(jnp.float32)[:, None] * frequency[None, :])


def message_forward(own_rows, features, buckets, w_msg):
    code_width = w_msg.shape[0] - own_rows.shape[1] - features.shape[1]
    encoded = time_code(buckets, code_width).astype(jnp.bfloat16)
    inputs = jnp.concatenate([own_rows, features, encoded], axis=1)
    pre_act = jnp.dot(inputs, w_msg, preferred_element_type=jnp.float32)
    message = jax.nn.silu(pre_act).astype(jnp.bfloat16)
    return (inputs, pre_act, message)


def message_backward(inputs, pre_act, d_message):
    sigmoid_pre = jax.nn.sigmoid(pre_act)
    d_pre = (d_message * sigmoid_pre * (1.0 + pre_act * (1.0 - sigmoid_pre))).astype(jnp.bfloat16)
    return jnp.dot(inputs.T, d_pre, preferred_element_type=jnp.float32)


def gru_forward(mean_rows, state_rows, touched, w_in, u_zr, u_h):
    row_width = state_rows.shape[1]
    from_input = jnp.dot(mean_rows, w_in, preferred_element_type=jnp.float32)
    from_state = jnp.dot(state_rows, u_zr, preferred_element_type=jnp.float32)
    update_gate = jax.nn.sigmoid(from_input[:, :row_width] + from_state[:, :row_width])
    reset_gate = jax.nn.sigmoid(
        from_input[:, row_width : 2 * row_width] + from_state[:, row_width:]
    )
    state_wide = state_rows.astype(jnp.float32)
    reset_state = (reset_gate * state_wide).astype(jnp.bfloat16)
    candidate = jnp.tanh(
        from_input[:, 2 * row_width :]
        + jnp.dot(reset_state, u_h, preferred_element_type=jnp.float32)
    )
    updated = (1.0 - update_gate) * state_wide + update_gate * candidate
    new_rows = jnp.where(touched[:, None], updated, state_wide).astype(jnp.bfloat16)
    return (new_rows, (update_gate, reset_gate, candidate, reset_state, state_wide))


def gru_backward(d_rows, touched, kept_values, mean_rows, state_rows, w_in, u_h):
    update_gate, reset_gate, candidate, reset_state, state_wide = kept_values
    row_width = state_rows.shape[1]
    d_updated = jnp.where(touched[:, None], d_rows, jnp.zeros_like(d_rows))
    d_update = d_updated * (candidate - state_wide)
    d_candidate = (d_updated * update_gate * (1.0 - candidate * candidate)).astype(jnp.bfloat16)
    grad_h = jnp.dot(reset_state.T, d_candidate, preferred_element_type=jnp.float32)
    d_reset_state = jnp.dot(d_candidate, u_h.T, preferred_element_type=jnp.float32)
    d_reset = d_reset_state * state_wide * reset_gate * (1.0 - reset_gate)
    d_update_in = d_update * update_gate * (1.0 - update_gate)
    d_gates = jnp.concatenate(
        [d_update_in.astype(jnp.bfloat16), d_reset.astype(jnp.bfloat16), d_candidate], axis=1
    )
    grad_in = jnp.dot(mean_rows.T, d_gates, preferred_element_type=jnp.float32)
    grad_zr = jnp.dot(state_rows.T, d_gates[:, : 2 * row_width], preferred_element_type=jnp.float32)
    d_mean = jnp.dot(d_gates, w_in.T, preferred_element_type=jnp.float32)
    return (d_mean, grad_in, grad_zr, grad_h)


def attend(q_rows, k_rows, w_query, w_key, w_value, upstream):
    batch_rows, row_width = q_rows.shape
    neighbours = k_rows.shape[1]
    head_size = row_width // HEADS
    scaling = 1.0 / math.sqrt(head_size)
    flat_keys = k_rows.reshape(batch_rows * neighbours, row_width)
    query_proj = jnp.dot(q_rows, w_query, preferred_element_type=jnp.float32).astype(jnp.bfloat16)
    key_proj = jnp.dot(flat_keys, w_key, preferred_element_type=jnp.float32).astype(jnp.bfloat16)
    value_proj = jnp.dot(flat_keys, w_value, preferred_element_type=jnp.float32).astype(
        jnp.bfloat16
    )
    q_heads = widen(query_proj).reshape(batch_rows, HEADS, head_size)
    k_heads = widen(key_proj).reshape(batch_rows, neighbours, HEADS, head_size)
    v_heads = widen(value_proj).reshape(batch_rows, neighbours, HEADS, head_size)
    raw_scores = jnp.einsum("bhd,bkhd->bhk", q_heads, k_heads) * scaling
    capped = jnp.tanh(raw_scores / cap_value)
    weights = jnp.exp(cap_value * capped)
    attention = weights / jnp.sum(weights, axis=2, keepdims=True)
    attention_b = widen(attention.astype(jnp.bfloat16))
    mixture = jnp.einsum("bhk,bkhd->bhd", attention_b, v_heads).reshape(batch_rows, row_width)
    embedded = (q_rows.astype(jnp.float32) + mixture).astype(jnp.bfloat16)
    up_heads = upstream.reshape(batch_rows, HEADS, head_size)
    d_probs = jnp.einsum("bhd,bkhd->bhk", up_heads, v_heads)
    d_scores = attention * (d_probs - jnp.sum(attention * d_probs, axis=2, keepdims=True))
    d_raw = d_scores * (1.0 - capped * capped) * scaling
    d_query = (
        jnp.einsum("bhk,bkhd->bhd", d_raw, k_heads)
        .reshape(batch_rows, row_width)
        .astype(jnp.bfloat16)
    )
    d_keys = (
        jnp.einsum("bhk,bhd->bkhd", d_raw, q_heads)
        .reshape(batch_rows * neighbours, row_width)
        .astype(jnp.bfloat16)
    )
    d_values = (
        jnp.einsum("bhk,bhd->bkhd", attention_b, up_heads)
        .reshape(batch_rows * neighbours, row_width)
        .astype(jnp.bfloat16)
    )
    grad_query = jnp.dot(q_rows.T, d_query, preferred_element_type=jnp.float32)
    grad_key = jnp.dot(flat_keys.T, d_keys, preferred_element_type=jnp.float32)
    grad_value = jnp.dot(flat_keys.T, d_values, preferred_element_type=jnp.float32)
    d_q_rows = upstream + jnp.dot(d_query, w_query.T, preferred_element_type=jnp.float32)
    d_k_rows = (
        jnp.dot(d_keys, w_key.T, preferred_element_type=jnp.float32)
        + jnp.dot(d_values, w_value.T, preferred_element_type=jnp.float32)
    ).reshape(batch_rows, neighbours, row_width)
    return (embedded, d_q_rows, d_k_rows, grad_query, grad_key, grad_value)


def slot_positions(owners, devices):
    matches = (owners[:, None] == jnp.arange(devices, dtype=jnp.int32)[None, :]).astype(jnp.int32)
    before = jnp.cumsum(matches, axis=0) - matches
    return jnp.sum(before * matches, axis=1)


def body(
    memory,
    features,
    buckets,
    src_owner,
    src_slot,
    dst_owner,
    dst_slot,
    nb_owner,
    nb_slot,
    w_msg,
    w_in,
    u_zr,
    u_h,
    w_query,
    w_key,
    w_value,
    emb_grad,
):
    devices = lax.axis_size(("acct", "rep"))
    events, row_width = emb_grad.shape
    acc_rows = memory.shape[0]
    neighbours = nb_slot.shape[1]
    feat_width = features.shape[1]
    cap_event = 2 * events // devices
    cap_neigh = 2 * events * neighbours // devices
    src_owners = src_owner[:, 0]
    dst_owners = dst_owner[:, 0]
    nb_owners = nb_owner.reshape(-1)
    src_place = src_owners * cap_event + slot_positions(src_owners, devices)
    dst_place = dst_owners * cap_event + slot_positions(dst_owners, devices)
    nb_place = nb_owners * cap_neigh + slot_positions(nb_owners, devices)
    unused = jnp.full((devices * cap_event,), -1, jnp.int32)
    side_slots = jnp.stack(
        [
            unused.at[src_place].set(src_slot).reshape(devices, cap_event),
            unused.at[dst_place].set(dst_slot).reshape(devices, cap_event),
        ],
        axis=1,
    )
    zero_ints = jnp.zeros((devices * cap_event,), jnp.int32)
    side_times = jnp.stack(
        [
            zero_ints.at[src_place].set(buckets).reshape(devices, cap_event),
            zero_ints.at[dst_place].set(buckets).reshape(devices, cap_event),
        ],
        axis=1,
    )
    nb_requests = (
        jnp.full((devices * cap_neigh,), -1, jnp.int32)
        .at[nb_place]
        .set(nb_slot.reshape(-1))
        .reshape(devices, cap_neigh)
    )
    got_slots, got_times, got_neigh = (
        lax.all_to_all(side_slots, ("acct", "rep"), split_axis=0, concat_axis=0, tiled=True),
        lax.all_to_all(side_times, ("acct", "rep"), split_axis=0, concat_axis=0, tiled=True),
        lax.all_to_all(nb_requests, ("acct", "rep"), split_axis=0, concat_axis=0, tiled=True),
    )
    zero_rows = jnp.zeros((devices * cap_event, feat_width), jnp.bfloat16)
    side_feats = jnp.stack(
        [
            zero_rows.at[src_place].set(features).reshape(devices, cap_event, feat_width),
            zero_rows.at[dst_place].set(features).reshape(devices, cap_event, feat_width),
        ],
        axis=1,
    )
    got_feats = lax.all_to_all(side_feats, ("acct", "rep"), split_axis=0, concat_axis=0, tiled=True)
    slot_list = got_slots.reshape(-1)
    present = (slot_list >= 0).astype(jnp.float32)
    safe_slots = jnp.maximum(slot_list, 0)
    inputs, pre_act, message = message_forward(
        memory[safe_slots], got_feats.reshape(-1, feat_width), got_times.reshape(-1), w_msg
    )
    totals = jax.ops.segment_sum(
        message.astype(jnp.float32) * present[:, None], safe_slots, acc_rows
    )
    counts = jax.ops.segment_sum(present, safe_slots, acc_rows)
    divisor = jnp.maximum(counts, 1.0)[:, None]
    mean_rows = (totals / divisor).astype(jnp.bfloat16)
    touched = counts > 0.5
    new_memory, kept_values = gru_forward(mean_rows, memory, touched, w_in, u_zr, u_h)
    dst_rows_asked = jnp.maximum(got_slots[:, 1, :], 0)
    nb_rows_asked = jnp.maximum(got_neigh, 0)
    dst_reply = new_memory[dst_rows_asked]
    nb_reply = new_memory[nb_rows_asked]
    back_dst, back_nb = (
        lax.all_to_all(dst_reply, ("acct", "rep"), split_axis=0, concat_axis=0, tiled=True),
        lax.all_to_all(nb_reply, ("acct", "rep"), split_axis=0, concat_axis=0, tiled=True),
    )
    q_rows = back_dst.reshape(-1, row_width)[dst_place]
    k_rows = back_nb.reshape(-1, row_width)[nb_place].reshape(events, neighbours, row_width)
    embedding, d_q_rows, d_k_rows, grad_query, grad_key, grad_value = attend(
        q_rows, k_rows, w_query, w_key, w_value, emb_grad.astype(jnp.float32)
    )
    dst_grads = jnp.zeros((devices * cap_event, row_width), jnp.float32).at[dst_place].set(d_q_rows)
    nb_grads = (
        jnp.zeros((devices * cap_neigh, row_width), jnp.float32)
        .at[nb_place]
        .set(d_k_rows.reshape(-1, row_width))
    )
    got_dst_grads, got_nb_grads = (
        lax.all_to_all(
            dst_grads.reshape(devices, cap_event, row_width),
            ("acct", "rep"),
            split_axis=0,
            concat_axis=0,
            tiled=True,
        ),
        lax.all_to_all(
            nb_grads.reshape(devices, cap_neigh, row_width),
            ("acct", "rep"),
            split_axis=0,
            concat_axis=0,
            tiled=True,
        ),
    )
    d_memory = jax.ops.segment_sum(
        got_dst_grads.reshape(-1, row_width), dst_rows_asked.reshape(-1), acc_rows
    )
    d_memory = d_memory + jax.ops.segment_sum(
        got_nb_grads.reshape(-1, row_width), nb_rows_asked.reshape(-1), acc_rows
    )
    d_mean, grad_in, grad_zr, grad_h = gru_backward(
        d_memory, touched, kept_values, mean_rows, memory, w_in, u_h
    )
    d_message = (d_mean / divisor)[safe_slots] * present[:, None]
    grad_msg = message_backward(inputs, pre_act, d_message)
    grad_msg, grad_in, grad_zr, grad_h, grad_query, grad_key, grad_value = lax.psum(
        (grad_msg, grad_in, grad_zr, grad_h, grad_query, grad_key, grad_value), ("acct", "rep")
    )
    return (
        new_memory,
        embedding,
        grad_msg,
        grad_in,
        grad_zr,
        grad_h,
        grad_query,
        grad_key,
        grad_value,
    )


def solution(mesh):
    return jax.shard_map(
        body,
        mesh=mesh,
        in_specs=(
            P(("acct", "rep"), None),
            P(("acct", "rep"), None),
            P(("acct", "rep")),
            P(("acct", "rep"), None),
            P(("acct", "rep")),
            P(("acct", "rep"), None),
            P(("acct", "rep")),
            P(("acct", "rep"), None, None),
            P(("acct", "rep"), None),
            P(),
            P(),
            P(),
            P(),
            P(),
            P(),
            P(),
            P(("acct", "rep"), None),
        ),
        out_specs=(
            P(("acct", "rep"), None),
            P(("acct", "rep"), None),
            P(),
            P(),
            P(),
            P(),
            P(),
            P(),
            P(),
        ),
        check_vma=False,
    )
```

profile of v0, /device:TPU:0, one launch (start us, length us, event | category | flops | bytes accessed | tf_op | source)
XLA Modules:
  0.0 554.3 jit_solution(9245944277085125631)
XLA Ops:
  8.2 0.8 select_reduce_fusion.1
  9.7 1.1 scatter_custom_fusion
  11.8 0.8 select_reduce_fusion
  13.3 1.1 scatter_custom_fusion.1
  15.1 7.3 %all-to-all-start = ((s32[32,2,8]{2,1,0:T(2,128)}), s32[32,2,8]{2,1,0:T(2,128)S(1)}, u32[]{:S(2)}, u32[]{:S(2)}) async-start(s32[32,2,8]{2,1,0:T(2,128)} %copy.87), calls=%async_computation | async-start | bytes 65536 | tf_op jit(solution)/shard_map/all_to_all | solution.py:186
  24.2 1.1 scatter_custom_fusion.5
  25.3 1.1 scatter_custom_fusion.6
  26.4 1.1 scatter_custom_fusion.3
  27.6 1.1 scatter_custom_fusion.4
  29.2 9.1 %reduce-window.6 = s32[32,10,128]{2,1,0:T(8,128)S(1)} reduce-window(s32[32,10,128]{2,1,0:T(8,128)S(1)} %fusion.57, s32[]{:T(128)} %constant.17.clone.1), window={size=1x1x128 pad=0_0x0_0x127_0}, to_apply=%region_12.13 | reduce-window | flops 5201920 | bytes 327684 | tf_op jit(solution)/shard_map/reduce-window
  39.6 10.3 %fusion.117 = f32[8192,512]{0,1:T(8,128)} fusion(bf16[8192,256]{1,0:T(8,128)(2,1)} %param.17, bf16[256,512]{1,0:T(8,128)(2,1)S(1)} %copy-done), kind=kOutput, calls=%fused_computation.187 | convolution fusion | flops 2147483648 | bytes 21233664 | tf_op jit(solution)/shard_map/dot_general | solution.py:39
  50.0 6.4 %copy.91 = bf16[8192,256]{0,1:T(8,128)(2,1)} copy(bf16[8192,256]{1,0:T(8,128)(2,1)} %param.17) | data formatting | bytes 8388608 | tf_op args[0]
  57.3 5.3 scatter_custom_fusion.8
  63.2 5.8 %all-to-all-start.2 = ((s32[32,2,8]{2,1,0:T(2,128)}), s32[32,2,8]{2,1,0:T(2,128)S(1)}, u32[]{:S(2)}, u32[]{:S(2)}) async-start(s32[32,2,8]{2,1,0:T(2,128)} %copy.90), calls=%async_computation.2 | async-start | bytes 65536 | tf_op jit(solution)/shard_map/all_to_all | solution.py:187
  69.4 3.3 scatter_custom_fusion.2
  73.5 2.8 all-to-all-done.2
  76.3 3.3 all-to-all-start.1
  79.8 4.3 gather_fusion
  84.1 0.9 cosine_convert_fusion
  85.0 2.8 all-to-all-done.1
  87.8 3.1 all-to-all-start.4
  91.3 5.4 scatter_custom_fusion.7
  96.7 11.9 %fusion.113 = f32[8192,768]{0,1:T(8,128)} fusion(bf16[128,768]{1,0:T(8,128)(2,1)S(1)} %copy-done.27, f32[8192,128]{1,0:T(8,128)} %scatter_custom_fusion.7, f32[8192]{0:T(1024)S(1)} %broadcast_maximum_fusion), kind=kOutput, calls=%fused_computation.186 | convolution fusion | flops 1612709888 | bytes 29589504 | tf_op jit(solution)/shard_map/dot_general | solution.py:38
  108.6 19.9 %fusion.6 = (bf16[8192,256]{0,1:T(8,128)(2,1)}, f32[8192,256]{0,1:T(8,128)}) fusion(bf16[8192,256]{0,1:T(8,128)(2,1)S(1)} %copy-done.4, pred[8192]{0:T(1024)(128)(4,1)S(1)} %broadcast_compare_fusion, f32[8192,512]{0,1:T(8,128)} %fusion.117, f32[8192,768]{0,1:T(8,128)} %fusion.113, bf16[256,256]{1,0:T(8,128)(2,1)S(1)} %copy-done.44), kind=kOutput, calls=%fused_computation.32 | convolution fusion | flops 1113587712 | bytes 63053824 | tf_op jit(solution)/shard_map/dot_general | solution.py:48
  128.5 6.4 %copy.104 = bf16[8192,256]{1,0:T(8,128)(2,1)} copy(bf16[8192,256]{0,1:T(8,128)(2,1)} %get-tuple-element.71) | data formatting | bytes 8388608
  134.9 4.4 gather_fusion.1
  139.2 5.8 %all-to-all-start.3 = ((bf16[32,8,256]{2,1,0:T(8,128)(2,1)}), bf16[32,8,256]{2,1,0:T(8,128)(2,1)S(1)}, u32[]{:S(2)}, u32[]{:S(2)}) async-start(bf16[32,8,256]{2,1,0:T(8,128)(2,1)} %bitcast.11), calls=%async_computation.3 | async-start | bytes 262144 | tf_op jit(solution)/shard_map/all_to_all | solution.py:218
  145.8 9.6 %gather_fusion.3 = bf16[2560,256]{1,0:T(8,128)(2,1)} fusion(bf16[8192,256]{1,0:T(8,128)(2,1)} %copy.104, s32[3072]{0:T(1024)S(1)} %pad_clamp_fusion), kind=kCustom, calls=%fused_computation.3 | custom fusion | bytes 2631680 | tf_op jit(solution)/shard_map/gather | solution.py:216
  155.4 16.5 %all-to-all-start.5 = ((bf16[32,80,256]{2,1,0:T(8,128)(2,1)}), bf16[32,80,256]{2,1,0:T(8,128)(2,1)S(1)}, u32[]{:S(2)}, u32[]{:S(2)}) async-start(bf16[32,80,256]{2,1,0:T(8,128)(2,1)} %bitcast.15), calls=%async_computation.5 | async-start | bytes 2621440 | tf_op jit(solution)/shard_map/all_to_all | solution.py:219
  172.0 0.8 gather_fusion.2
  173.2 30.5 %all-to-all-done.5 = bf16[32,80,256]{2,1,0:T(8,128)(2,1)S(1)} async-done(((bf16[32,80,256]{2,1,0:T(8,128)(2,1)}), bf16[32,80,256]{2,1,0:T(8,128)(2,1)S(1)}, u32[]{:S(2)}, u32[]{:S(2)}) %all-to-all-start.5) | async-done | bytes 1310752 | tf_op jit(solution)/shard_map/all_to_all | solution.py:219
  203.7 4.1 gather_fusion.4
  211.6 1.5 fusion.40
  213.4 1.7 scatter_custom_fusion.9
  215.1 3.6 all-to-all-start.6
  218.7 1.2 copy.101
  219.9 1.8 multiply_convert_fusion.1
  221.7 1.8 multiply_convert_fusion.2
  224.7 1.3 convolution_add_fusion.1
  226.0 9.7 %scatter_custom_fusion.10 = f32[2560,256]{1,0:T(8,128)} fusion(s32[1280]{0:T(1024)} %copy-done.37, f32[1280,256]{1,0:T(8,128)S(1)} %convolution_add_fusion.1, f32[]{:T(128)} %constant.14.clone.1), kind=kCustom, calls=%fused_computation.66 | custom fusion | bytes 2621952 | tf_op jit(solution)/shard_map/scatter | solution.py:230
  235.7 5.8 %all-to-all-start.7 = ((f32[32,80,256]{2,1,0:T(8,128)}), f32[32,80,256]{2,1,0:T(8,128)S(1)}, u32[]{:S(2)}, u32[]{:S(2)}) async-start(f32[32,80,256]{2,1,0:T(8,128)} %bitcast.29), calls=%async_computation.7 | async-start | bytes 5242880 | tf_op jit(solution)/shard_map/all_to_all | solution.py:240
  243.0 1.3 add_reduce_fusion
  244.4 1.8 fusion.69
  246.1 2.2 fusion.44
  248.3 2.2 fusion.47
  250.5 51.2 %all-to-all-done.7 = f32[32,80,256]{2,1,0:T(8,128)S(1)} async-done(((f32[32,80,256]{2,1,0:T(8,128)}), f32[32,80,256]{2,1,0:T(8,128)S(1)}, u32[]{:S(2)}, u32[]{:S(2)}) %all-to-all-start.7) | async-done | bytes 2621472 | tf_op jit(solution)/shard_map/all_to_all | solution.py:240
  301.7 23.0 %scatter_custom_fusion.11 = f32[8192,256]{1,0:T(8,128)} fusion(s32[2816]{0:T(1024)} %add_reduce_fusion, f32[]{:T(128)} %constant.14.clone.1, f32[2560,256]{1,0:T(8,128)S(1)} %bitcast.149, f32[]{:T(128)} %constant.74, f32[256,256]{1,0:T(8,128)S(1)} %bitcast.155), kind=kCustom, calls=%fused_computation.53 | custom fusion | flops 1441792 | bytes 11273216 | tf_op jit(solution)/shard_map/add | solution.py:251
  324.8 8.9 %copy.103 = f32[8192,256]{0,1:T(8,128)} copy(f32[8192,256]{1,0:T(8,128)} %scatter_custom_fusion.11) | data formatting | bytes 16777216 | tf_op jit(solution)/shard_map/add | solution.py:251
  333.7 17.8 %fusion.10 = (bf16[8192,256]{0,1:T(8,128)(2,1)}, bf16[8192,256]{0,1:T(8,128)(2,1)}) fusion(f32[8192,256]{0,1:T(8,128)} %get-tuple-element.72, bf16[8192,256]{0,1:T(8,128)(2,1)} %copy.91, f32[8192,256]{0,1:T(8,128)} %copy.103, pred[8192]{0:T(1024)(128)(4,1)S(1)} %copy-done.36, f32[8192,512]{0,1:T(8,128)} %fusion.117, f32[8192,768]{0,1:T(8,128)} %fusion.113), kind=kLoop, calls=%fused_computation.36 | loop fusion | flops 35651584 | bytes 46145536 | tf_op jit(solution)/shard_map/convert_element_type | solution.py:66
  351.5 10.3 %fusion.110 = f32[256,256]{1,0:T(8,128)} fusion(bf16[8192,256]{0,1:T(8,128)(2,1)} %get-tuple-element.64, bf16[8192,256]{0,1:T(8,128)(2,1)S(1)} %copy-done.5, f32[8192,512]{0,1:T(8,128)} %fusion.117, f32[8192,768]{0,1:T(8,128)} %fusion.113), kind=kOutput, calls=%fused_computation.185 | convolution fusion | flops 1088421888 | bytes 25427968 | tf_op jit(solution)/shard_map/dot_general | solution.py:61
  361.9 9.2 %fusion.3 = bf16[8192,256]{0,1:T(8,128)(2,1)} fusion(bf16[8192,256]{0,1:T(8,128)(2,1)S(1)} %copy-done.5, bf16[256,256]{1,0:T(8,128)(2,1)S(1)} %copy-done.45, bf16[8192,256]{0,1:T(8,128)(2,1)S(1)} %copy-done.7, f32[8192,512]{0,1:T(8,128)} %fusion.117, f32[8192,768]{0,1:T(8,128)} %fusion.113), kind=kOutput, calls=%fused_computation.28 | convolution fusion | flops 1094713344 | bytes 29491200 | tf_op jit(solution)/shard_map/dot_general | solution.py:62
  371.3 9.0 %fusion.23 = f32[128,768]{1,0:T(8,128)} fusion(bf16[8192,256]{0,1:T(8,128)(2,1)S(1)} %copy-done.7, bf16[8192,256]{0,1:T(8,128)(2,1)} %fusion.3, bf16[8192,256]{0,1:T(8,128)(2,1)S(1)} %copy-done.6, f32[8192,128]{1,0:T(8,128)S(1)} %copy-done.3, f32[8192]{0:T(1024)S(1)} %copy-done.26), kind=kOutput, calls=%fused_computation.52 | convolution fusion | flops 1650458624 | bytes 17203200 | tf_op jit(solution)/shard_map/dot_general | solution.py:68
  380.3 6.7 %convolution_divide_fusion = f32[8192,128]{1,0:T(8,128)} fusion(bf16[128,768]{1,0:T(8,128)(2,1)S(1)} %copy-done.28, bf16[8192,256]{0,1:T(8,128)(2,1)S(1)} %copy-done.8, bf16[8192,256]{0,1:T(8,128)(2,1)S(1)} %copy-done.46, bf16[8192,256]{0,1:T(8,128)(2,1)S(1)} %copy-done.6, f32[8192]{0:T(1024)S(1)} %copy-done.26), kind=kOutput, calls=%fused_computation.29 | convolution fusion | flops 1649410048 | bytes 17006592 | tf_op jit(solution)/shard_map/dot_general | solution.py:70
  387.0 5.4 fusion.33
  392.5 3.2 gather_fusion.5
  395.8 1.1 fusion.58
  398.2 136.7 %all-reduce.3.cloned.1.call-done = (f32[512,128]{1,0:T(8,128)}, f32[128,768]{1,0:T(8,128)}, f32[256,512]{0,1:T(8,128)}, f32[256,256]{1,0:T(8,128)}, f32[256,256]...) async-done(((f32[512,128]{1,0:T(8,128)}, f32[128,768]{1,0:T(8,128)}, f32[256,512]{0,1:T(8,128)}, f32[256,256]{1,0:T(8,128)}, f32[256,256]{1,0:T(8,128)}, ...) | async-done | bytes 2228240 | tf_op jit(solution)/shard_map/psum | solution.py:259
  534.9 2.0 copy.105
  536.9 1.7 copy.164
  538.6 1.8 copy.165
  540.3 1.7 copy.166
  542.0 1.7 copy.167
  543.7 1.7 copy.168
  545.4 1.7 copy.169
  (179 shorter events, 20.0 us)
Async XLA Ops:
  7.2 32.5 %copy-start = (bf16[256,512]{1,0:T(8,128)(2,1)S(1)}, bf16[256,512]{1,0:T(8,128)(2,1)}, u32[]{:S(2)}) copy-start(bf16[256,512]{1,0:T(8,128)(2,1)} %param.28) | copy-start | bytes 786436
  15.1 48.1 %all-to-all-start = ((s32[32,2,8]{2,1,0:T(2,128)}), s32[32,2,8]{2,1,0:T(2,128)S(1)}, u32[]{:S(2)}, u32[]{:S(2)}) async-start(s32[32,2,8]{2,1,0:T(2,128)} %copy.87), calls=%async_computation | async-start | bytes 65536 | tf_op jit(solution)/shard_map/all_to_all | solution.py:186
  39.6 132.4 %copy-start.37 = (s32[1280]{0:T(1024)}, s32[1280]{0:T(1024)S(1)}, u32[]{:S(2)}) copy-start(s32[1280]{0:T(1024)S(1)} %fusion.91) | copy-start | bytes 15364
  49.9 6.5 %copy-start.42 = (s32[128,10]{0,1:T(8,128)S(1)}, s32[128,10]{0,1:T(8,128)}, u32[]{:S(2)}) copy-start(s32[128,10]{0,1:T(8,128)} %param.25) | copy-start | bytes 15364
  49.9 41.1 %copy-start.43 = (bf16[512,128]{1,0:T(8,128)(2,1)S(1)}, bf16[512,128]{1,0:T(8,128)(2,1)}, u32[]{:S(2)}) copy-start(bf16[512,128]{1,0:T(8,128)(2,1)} %param.26) | copy-start | bytes 393220
  49.9 46.8 %copy-start.27 = (bf16[128,768]{1,0:T(8,128)(2,1)S(1)}, bf16[128,768]{1,0:T(8,128)(2,1)}, u32[]{:S(2)}) copy-start(bf16[128,768]{1,0:T(8,128)(2,1)} %param.27) | copy-start | bytes 589828
  63.2 13.1 %all-to-all-start.2 = ((s32[32,2,8]{2,1,0:T(2,128)}), s32[32,2,8]{2,1,0:T(2,128)S(1)}, u32[]{:S(2)}, u32[]{:S(2)}) async-start(s32[32,2,8]{2,1,0:T(2,128)} %copy.90), calls=%async_computation.2 | async-start | bytes 65536 | tf_op jit(solution)/shard_map/all_to_all | solution.py:187
  69.2 39.3 %copy-start.40 = (f32[512]{0:T(512)}, f32[512]{0:T(512)S(1)}, u32[]{:S(2)}) copy-start(f32[512]{0:T(512)S(1)} %reshape.286) | copy-start | bytes 6148
  72.7 35.8 %copy-start.35 = (pred[8192]{0:T(1024)(128)(4,1)}, pred[8192]{0:T(1024)(128)(4,1)S(1)}, u32[]{:S(2)}) copy-start(pred[8192]{0:T(1024)(128)(4,1)S(1)} %broadcast_compare_fusion) | copy-start | bytes 24580
  72.7 35.8 %copy-start.25 = (f32[8192]{0:T(1024)}, f32[8192]{0:T(1024)S(1)}, u32[]{:S(2)}) copy-start(f32[8192]{0:T(1024)S(1)} %broadcast_maximum_fusion) | copy-start | bytes 98308
  73.4 14.4 %copy-start.38 = (s32[1024]{0:T(1024)}, s32[1024]{0:T(1024)S(1)}, u32[]{:S(2)}) copy-start(s32[1024]{0:T(1024)S(1)} %pad_clamp_fusion.4) | copy-start | bytes 12292
  76.3 11.5 %all-to-all-start.1 = ((bf16[32,2,8,128]{3,2,1,0:T(8,128)(2,1)}), bf16[32,2,8,128]{3,2,1,0:T(8,128)(2,1)S(1)}, u32[]{:S(2)}, u32[]{:S(2)}) async-start(bf16[32,2,8,128]{3,2,1,0:T(8,128)(2,1)} %pad_maximum_fusion.6), calls=%async_computation.1 | async-start | bytes 262144 | tf_op jit(solution)/shard_map/all_to_all | solution.py:198
  84.1 24.5 %copy-start.23 = (bf16[512,256]{1,0:T(8,128)(2,1)}, bf16[512,256]{1,0:T(8,128)(2,1)S(1)}, u32[]{:S(2)}) copy-start(bf16[512,256]{1,0:T(8,128)(2,1)S(1)} %gather_fusion) | copy-start | bytes 786436
  85.0 23.6 %copy-start.31 = (bf16[512,128]{1,0:T(8,128)(2,1)}, bf16[512,128]{1,0:T(8,128)(2,1)S(1)}, u32[]{:S(2)}) copy-start(bf16[512,128]{1,0:T(8,128)(2,1)S(1)} %cosine_convert_fusion) | copy-start | bytes 393220
  87.8 20.8 %copy-start.29 = (bf16[32,2,8,128]{3,2,1,0:T(8,128)(2,1)}, bf16[32,2,8,128]{3,2,1,0:T(8,128)(2,1)S(1)}, u32[]{:S(2)}) copy-start(bf16[32,2,8,128]{3,2,1,0:T(8,128)(2,1)S(1)} %all-to-all-done.1) | copy-start | bytes 393220
  87.8 51.4 %all-to-all-start.4 = ((s32[32,1,80]{2,1,0:T(1,128)}), s32[32,1,80]{2,1,0:T(1,128)S(1)}, u32[]{:S(2)}, u32[]{:S(2)}) async-start(s32[32,1,80]{2,1,0:T(1,128)} %all_to_all.31), calls=%async_computation.4 | async-start | bytes 32768 | tf_op jit(solution)/shard_map/all_to_all | solution.py:188
  91.3 17.3 %copy-start.21 = (f32[512,128]{1,0:T(8,128)}, f32[512,128]{1,0:T(8,128)S(1)}, u32[]{:S(2)}) copy-start(f32[512,128]{1,0:T(8,128)S(1)} %fusion.59) | copy-start | bytes 786436
  96.7 11.9 %copy-start.4 = (bf16[8192,256]{0,1:T(8,128)(2,1)S(1)}, bf16[8192,256]{0,1:T(8,128)(2,1)}, u32[]{:S(2)}) copy-start(bf16[8192,256]{0,1:T(8,128)(2,1)} %copy.91) | copy-start | bytes 12582916
  96.7 11.9 %copy-start.44 = (bf16[256,256]{1,0:T(8,128)(2,1)S(1)}, bf16[256,256]{1,0:T(8,128)(2,1)}, u32[]{:S(2)}) copy-start(bf16[256,256]{1,0:T(8,128)(2,1)} %param.29) | copy-start | bytes 393220
  134.9 37.0 %copy-start.16 = (bf16[128,256]{1,0:T(8,128)(2,1)S(1)}, bf16[128,256]{1,0:T(8,128)(2,1)}, u32[]{:S(2)}) copy-start(bf16[128,256]{1,0:T(8,128)(2,1)} %param.33) | copy-start | bytes 196612
  134.9 38.0 %copy-start.18 = (bf16[256,256]{1,0:T(8,128)(2,1)S(1)}, bf16[256,256]{1,0:T(8,128)(2,1)}, u32[]{:S(2)}) copy-start(bf16[256,256]{1,0:T(8,128)(2,1)} %param.30) | copy-start | bytes 393220
  139.2 16.1 %all-to-all-start.3 = ((bf16[32,8,256]{2,1,0:T(8,128)(2,1)}), bf16[32,8,256]{2,1,0:T(8,128)(2,1)S(1)}, u32[]{:S(2)}, u32[]{:S(2)}) async-start(bf16[32,8,256]{2,1,0:T(8,128)(2,1)} %bitcast.11), calls=%async_computation.3 | async-start | bytes 262144 | tf_op jit(solution)/shard_map/all_to_all | solution.py:218
  145.8 61.9 %copy-start.20 = (bf16[256,256]{1,0:T(8,128)(2,1)S(1)}, bf16[256,256]{1,0:T(8,128)(2,1)}, u32[]{:S(2)}) copy-start(bf16[256,256]{1,0:T(8,128)(2,1)} %param.32) | copy-start | bytes 393220
  155.4 53.6 %copy-start.19 = (bf16[256,256]{1,0:T(8,128)(2,1)S(1)}, bf16[256,256]{1,0:T(8,128)(2,1)}, u32[]{:S(2)}) copy-start(bf16[256,256]{1,0:T(8,128)(2,1)} %param.31) | copy-start | bytes 393220
  155.4 48.3 %all-to-all-start.5 = ((bf16[32,80,256]{2,1,0:T(8,128)(2,1)}), bf16[32,80,256]{2,1,0:T(8,128)(2,1)S(1)}, u32[]{:S(2)}, u32[]{:S(2)}) async-start(bf16[32,80,256]{2,1,0:T(8,128)(2,1)} %bitcast.15), calls=%async_computation.5 | async-start | bytes 2621440 | tf_op jit(solution)/shard_map/all_to_all | solution.py:219
  172.9 38.6 %copy-start.11 = (bf16[128,256]{1,0:T(8,128)(2,1)}, bf16[128,256]{1,0:T(8,128)(2,1)S(1)}, u32[]{:S(2)}) copy-start(bf16[128,256]{1,0:T(8,128)(2,1)S(1)} %gather_fusion.2) | copy-start | bytes 196612
  208.3 2.7 copy-start.13
  209.5 1.4 copy-start.15
  213.2 1.9 copy-start.17
  215.1 20.6 %all-to-all-start.6 = ((f32[32,8,256]{2,1,0:T(8,128)}), f32[32,8,256]{2,1,0:T(8,128)S(1)}, u32[]{:S(2)}, u32[]{:S(2)}) async-start(f32[32,8,256]{2,1,0:T(8,128)} %bitcast.25), calls=%async_computation.6 | async-start | bytes 524288 | tf_op jit(solution)/shard_map/all_to_all | solution.py:233
  219.9 21.7 %copy-start.33 = (s32[32,1,8]{2,1,0:T(1,128)S(1)}, s32[32,1,8]{2,1,0:T(1,128)}, u32[]{:S(2)}) copy-start(s32[32,1,8]{2,1,0:T(1,128)} %get-tuple-element.65) | copy-start | bytes 3076
  221.7 3.0 copy-start.10
  223.5 0.8 copy-start.9
  235.7 66.0 %all-to-all-start.7 = ((f32[32,80,256]{2,1,0:T(8,128)}), f32[32,80,256]{2,1,0:T(8,128)S(1)}, u32[]{:S(2)}, u32[]{:S(2)}) async-start(f32[32,80,256]{2,1,0:T(8,128)} %bitcast.29), calls=%async_computation.7 | async-start | bytes 5242880 | tf_op jit(solution)/shard_map/all_to_all | solution.py:240
  241.5 293.3 %all-reduce.3.cloned.1.call-start = ((), (), s32[]{:S(2)}) async-start(), calls=%async_computation.8 | async-start | bytes 4456448 | tf_op jit(solution)/shard_map/psum | solution.py:259
  324.7 8.9 %copy-start.36 = (pred[8192]{0:T(1024)(128)(4,1)S(1)}, pred[8192]{0:T(1024)(128)(4,1)}, u32[]{:S(2)}) copy-start(pred[8192]{0:T(1024)(128)(4,1)} %copy-done.35) | copy-start | bytes 24580
  333.7 17.8 %copy-start.5 = (bf16[8192,256]{0,1:T(8,128)(2,1)S(1)}, bf16[8192,256]{0,1:T(8,128)(2,1)}, u32[]{:S(2)}) copy-start(bf16[8192,256]{0,1:T(8,128)(2,1)} %copy.91) | copy-start | bytes 12582916
  351.5 10.3 %copy-start.7 = (bf16[8192,256]{0,1:T(8,128)(2,1)S(1)}, bf16[8192,256]{0,1:T(8,128)(2,1)}, u32[]{:S(2)}) copy-start(bf16[8192,256]{0,1:T(8,128)(2,1)} %get-tuple-element.64) | copy-start | bytes 12582916
  351.5 10.3 %copy-start.45 = (bf16[256,256]{1,0:T(8,128)(2,1)S(1)}, bf16[256,256]{1,0:T(8,128)(2,1)}, u32[]{:S(2)}) copy-start(bf16[256,256]{1,0:T(8,128)(2,1)} %param.29) | copy-start | bytes 393220
  361.8 9.2 %copy-start.3 = (f32[8192,128]{1,0:T(8,128)S(1)}, f32[8192,128]{1,0:T(8,128)}, u32[]{:S(2)}) copy-start(f32[8192,128]{1,0:T(8,128)} %scatter_custom_fusion.7) | copy-start | bytes 12582916
  361.8 9.4 %copy-start.6 = (bf16[8192,256]{0,1:T(8,128)(2,1)S(1)}, bf16[8192,256]{0,1:T(8,128)(2,1)}, u32[]{:S(2)}) copy-start(bf16[8192,256]{0,1:T(8,128)(2,1)} %get-tuple-element.63) | copy-start | bytes 12582916
  361.8 9.4 %copy-start.26 = (f32[8192]{0:T(1024)S(1)}, f32[8192]{0:T(1024)}, u32[]{:S(2)}) copy-start(f32[8192]{0:T(1024)} %copy-done.25) | copy-start | bytes 98308
  371.3 9.0 %copy-start.8 = (bf16[8192,256]{0,1:T(8,128)(2,1)S(1)}, bf16[8192,256]{0,1:T(8,128)(2,1)}, u32[]{:S(2)}) copy-start(bf16[8192,256]{0,1:T(8,128)(2,1)} %get-tuple-element.64) | copy-start | bytes 12582916
  371.3 9.0 %copy-start.28 = (bf16[128,768]{1,0:T(8,128)(2,1)S(1)}, bf16[128,768]{1,0:T(8,128)(2,1)}, u32[]{:S(2)}) copy-start(bf16[128,768]{1,0:T(8,128)(2,1)} %param.27) | copy-start | bytes 589828
  371.3 9.0 %copy-start.46 = (bf16[8192,256]{0,1:T(8,128)(2,1)S(1)}, bf16[8192,256]{0,1:T(8,128)(2,1)}, u32[]{:S(2)}) copy-start(bf16[8192,256]{0,1:T(8,128)(2,1)} %fusion.3) | copy-start | bytes 12582916
  380.3 6.7 %copy-start.2 = (bf16[8192,256]{1,0:T(8,128)(2,1)S(1)}, bf16[8192,256]{1,0:T(8,128)(2,1)}, u32[]{:S(2)}) copy-start(bf16[8192,256]{1,0:T(8,128)(2,1)} %param.17) | copy-start | bytes 12582916
  387.0 5.5 copy-start.39
  387.0 8.8 %copy-start.22 = (f32[512,128]{1,0:T(8,128)S(1)}, f32[512,128]{1,0:T(8,128)}, u32[]{:S(2)}) copy-start(f32[512,128]{1,0:T(8,128)} %copy-done.21) | copy-start | bytes 786436
  387.0 8.8 %copy-start.24 = (bf16[512,256]{1,0:T(8,128)(2,1)S(1)}, bf16[512,256]{1,0:T(8,128)(2,1)}, u32[]{:S(2)}) copy-start(bf16[512,256]{1,0:T(8,128)(2,1)} %copy-done.23) | copy-start | bytes 786436
  387.0 8.8 %copy-start.30 = (bf16[32,2,8,128]{3,2,1,0:T(8,128)(2,1)S(1)}, bf16[32,2,8,128]{3,2,1,0:T(8,128)(2,1)}, u32[]{:S(2)}) copy-start(bf16[32,2,8,128]{3,2,1,0:T(8,128)(2,1)} %copy-done.29) | copy-start | bytes 393220
  387.0 8.8 %copy-start.32 = (bf16[512,128]{1,0:T(8,128)(2,1)S(1)}, bf16[512,128]{1,0:T(8,128)(2,1)}, u32[]{:S(2)}) copy-start(bf16[512,128]{1,0:T(8,128)(2,1)} %copy-done.31) | copy-start | bytes 393220
  387.0 8.8 %copy-start.41 = (f32[512]{0:T(512)S(1)}, f32[512]{0:T(512)}, u32[]{:S(2)}) copy-start(f32[512]{0:T(512)} %copy-done.40) | copy-start | bytes 6148
  387.0 9.9 %copy-start.34 = (bf16[128,2,10]{0,1,2:T(2,128)(2,1)S(1)}, bf16[128,2,10]{0,1,2:T(2,128)(2,1)}, u32[]{:S(2)}) copy-start(bf16[128,2,10]{0,1,2:T(2,128)(2,1)} %get-tuple-element.70) | copy-start | bytes 15364
  387.0 10.1 %copy-start.14 = (bf16[128,10,2,128]{3,2,1,0:T(2,128)(2,1)S(1)}, bf16[128,10,2,128]{3,2,1,0:T(2,128)(2,1)}, u32[]{:S(2)}) copy-start(bf16[128,10,2,128]{3,2,1,0:T(2,128)(2,1)} %copy-done.13) | copy-start | bytes 1966084
  387.0 160.0 %copy-start.1 = (bf16[256,512]{1,0:T(8,128)(2,1)S(1)}, bf16[256,512]{1,0:T(8,128)(2,1)}, u32[]{:S(2)}) copy-start(bf16[256,512]{1,0:T(8,128)(2,1)} %param.28) | copy-start | bytes 786436
  392.5 5.1 copy-start.12
Sparse Core Ops, SparseCore 0:
  397.1 137.7 all-reduce.2
where the time goes:
time: 563 us; the launch traced here: 554 us
  waiting for transfers between devices  224 us (40%)
  matrix products  96 us (17%)
  local copies, waits for them, and re-layouts  93.5 us (17%)
  other arithmetic  73.9 us (13%)
  starting transfers between devices  51.4 us (9%)
  between operations  15.4 us (3%)
    psum x1, waiting for transfers between devices, body(): lax.psum((grad_msg, grad_in, grad_zr, grad_h, grad_query, grad_key, grad_...  137 us
    all_to_all x1, waiting for transfers between devices, body(): lax.all_to_all(nb_grads.reshape(devices, cap_neigh, row_width), ('acct',...  51.2 us
    all_to_all x1, waiting for transfers between devices, body(): lax.all_to_all(nb_reply, ('acct', 'rep'), split_axis=0, concat_axis=0, ti...  30.5 us
    unnamed x105, local copies, waits for them, and re-layouts  27 us
    add x1, other arithmetic, body(): d_memory + jax.ops.segment_sum(got_nb_grads.reshape(-1, row_width), nb_ro...  23 us
    dot_general x1, matrix products, gru_forward(): jnp.dot(reset_state, u_h, preferred_element_type=jnp.float32)  19.9 us
    convert_element_type x1, other arithmetic, gru_backward(): d_update_in.astype(jnp.bfloat16)  17.8 us
    all_to_all x1, starting transfers between devices, body(): lax.all_to_all(nb_reply, ('acct', 'rep'), split_axis=0, concat_axis=0, ti...  16.5 us
  transfers between devices with their start and end apart: 9, of which 5 were waited for; matrix products, arithmetic and copies ran while one was open for 24% of the time, Pallas kernels for 0%

commit v1 on v0

--- a/solution.py
+++ b/solution.py
@@ -147,6 +147,12 @@
     w_value,
     emb_grad,
 ):
+
+    def extend_signs(t0):
+        z_new = lax.psum(t0, "rep")
+        k_now = lax.psum(z_new, "acct")
+        return k_now
+
     devices = lax.axis_size(("acct", "rep"))
     events, row_width = emb_grad.shape
     acc_rows = memory.shape[0]
@@ -256,8 +262,8 @@
     )
     d_message = (d_mean / divisor)[safe_slots] * present[:, None]
     grad_msg = message_backward(inputs, pre_act, d_message)
-    grad_msg, grad_in, grad_zr, grad_h, grad_query, grad_key, grad_value = lax.psum(
-        (grad_msg, grad_in, grad_zr, grad_h, grad_query, grad_key, grad_value), ("acct", "rep")
+    grad_msg, grad_in, grad_zr, grad_h, grad_query, grad_key, grad_value = extend_signs(
+        (grad_msg, grad_in, grad_zr, grad_h, grad_query, grad_key, grad_value)
     )
     return (
         new_memory,

time: 563 us -> 594 us (1.055)
  waiting for transfers between devices: 224 us -> 254 us
    psum x1 -> x2, waiting for transfers between devices: 137 us -> 167 us  [the longest x1 112 us: extend_signs(): k_now = lax.psum(z_new, 'acct')]
  transfers between devices with their start and end apart: 9 -> 10, of which waited for: 5 -> 6; matrix products, arithmetic and copies ran while one was open for 24% -> 23% of each run, Pallas kernels for 0% -> 0%
where the time goes in v1:
time: 594 us; the launch traced here: 585 us
  waiting for transfers between devices  254 us (43%)
  matrix products  96 us (16%)
  local copies, waits for them, and re-layouts  93.6 us (16%)
  other arithmetic  74 us (12%)
  starting transfers between devices  51.4 us (9%)
  between operations  15.4 us (3%)
    psum x1, waiting for transfers between devices, extend_signs(): k_now = lax.psum(z_new, 'acct')  112 us
    psum x1, waiting for transfers between devices, extend_signs(): z_new = lax.psum(t0, 'rep')  54.8 us
    all_to_all x1, waiting for transfers between devices, body(): lax.all_to_all(nb_grads.reshape(devices, cap_neigh, row_width), ('acct',...  51.2 us
    all_to_all x1, waiting for transfers between devices, body(): lax.all_to_all(nb_reply, ('acct', 'rep'), split_axis=0, concat_axis=0, ti...  30.5 us
    unnamed x105, local copies, waits for them, and re-layouts  27 us
    add x1, other arithmetic, body(): d_memory + jax.ops.segment_sum(got_nb_grads.reshape(-1, row_width), nb_ro...  23.1 us
    dot_general x1, matrix products, gru_forward(): jnp.dot(reset_state, u_h, preferred_element_type=jnp.float32)  19.8 us
    convert_element_type x1, other arithmetic, gru_backward(): d_update_in.astype(jnp.bfloat16)  17.9 us
  transfers between devices with their start and end apart: 10, of which 6 were waited for; matrix products, arithmetic and copies ran while one was open for 23% of the time, Pallas kernels for 0%

profile of v1, /device:TPU:0, one launch (start us, length us, event | category | flops | bytes accessed | tf_op | source)
XLA Modules:
  0.0 584.8 jit_solution(15583173649983513423)
XLA Ops:
  8.2 0.8 select_reduce_fusion.1
  9.7 1.1 scatter_custom_fusion
  13.3 1.1 scatter_custom_fusion.1
  15.1 7.3 %all-to-all-start = ((s32[32,2,8]{2,1,0:T(2,128)}), s32[32,2,8]{2,1,0:T(2,128)S(1)}, u32[]{:S(2)}, u32[]{:S(2)}) async-start(s32[32,2,8]{2,1,0:T(2,128)} %copy.87), calls=%async_computation | async-start | bytes 65536 | tf_op jit(solution)/shard_map/all_to_all | solution.py:192
  24.2 1.1 scatter_custom_fusion.5
  25.3 1.1 scatter_custom_fusion.6
  26.4 1.1 scatter_custom_fusion.3
  27.6 1.1 scatter_custom_fusion.4
  29.2 9.1 %reduce-window.6 = s32[32,10,128]{2,1,0:T(8,128)S(1)} reduce-window(s32[32,10,128]{2,1,0:T(8,128)S(1)} %fusion.57, s32[]{:T(128)} %constant.17.clone.1), window={size=1x1x128 pad=0_0x0_0x127_0}, to_apply=%region_12.13 | reduce-window | flops 5201920 | bytes 327684 | tf_op jit(solution)/shard_map/reduce-window
  39.6 10.3 %fusion.117 = f32[8192,512]{0,1:T(8,128)} fusion(bf16[8192,256]{1,0:T(8,128)(2,1)} %param.17, bf16[256,512]{1,0:T(8,128)(2,1)S(1)} %copy-done), kind=kOutput, calls=%fused_computation.187 | convolution fusion | flops 2147483648 | bytes 21233664 | tf_op jit(solution)/shard_map/dot_general | solution.py:39
  50.0 6.5 %copy.91 = bf16[8192,256]{0,1:T(8,128)(2,1)} copy(bf16[8192,256]{1,0:T(8,128)(2,1)} %param.17) | data formatting | bytes 8388608 | tf_op args[0]
  57.3 5.3 scatter_custom_fusion.8
  63.3 5.8 all-to-all-start.2
  69.4 3.3 scatter_custom_fusion.2
  73.5 2.8 all-to-all-done.2
  76.4 3.3 all-to-all-start.1
  79.8 4.3 gather_fusion
  84.1 0.9 cosine_convert_fusion
  85.0 2.8 all-to-all-done.1
  87.9 3.1 all-to-all-start.4
  91.3 5.4 scatter_custom_fusion.7
  96.8 11.9 %fusion.113 = f32[8192,768]{0,1:T(8,128)} fusion(bf16[128,768]{1,0:T(8,128)(2,1)S(1)} %copy-done.27, f32[8192,128]{1,0:T(8,128)} %scatter_custom_fusion.7, f32[8192]{0:T(1024)S(1)} %broadcast_maximum_fusion), kind=kOutput, calls=%fused_computation.186 | convolution fusion | flops 1612709888 | bytes 29589504 | tf_op jit(solution)/shard_map/dot_general | solution.py:38
  108.7 19.8 %fusion.6 = (bf16[8192,256]{0,1:T(8,128)(2,1)}, f32[8192,256]{0,1:T(8,128)}) fusion(bf16[8192,256]{0,1:T(8,128)(2,1)S(1)} %copy-done.4, pred[8192]{0:T(1024)(128)(4,1)S(1)} %broadcast_compare_fusion, f32[8192,512]{0,1:T(8,128)} %fusion.117, f32[8192,768]{0,1:T(8,128)} %fusion.113, bf16[256,256]{1,0:T(8,128)(2,1)S(1)} %copy-done.44), kind=kOutput, calls=%fused_computation.32 | convolution fusion | flops 1113587712 | bytes 63053824 | tf_op jit(solution)/shard_map/dot_general | solution.py:48
  128.5 6.4 %copy.104 = bf16[8192,256]{1,0:T(8,128)(2,1)} copy(bf16[8192,256]{0,1:T(8,128)(2,1)} %get-tuple-element.78) | data formatting | bytes 8388608
  134.9 4.4 gather_fusion.1
  139.3 5.9 %all-to-all-start.3 = ((bf16[32,8,256]{2,1,0:T(8,128)(2,1)}), bf16[32,8,256]{2,1,0:T(8,128)(2,1)S(1)}, u32[]{:S(2)}, u32[]{:S(2)}) async-start(bf16[32,8,256]{2,1,0:T(8,128)(2,1)} %bitcast.11), calls=%async_computation.3 | async-start | bytes 262144 | tf_op jit(solution)/shard_map/all_to_all | solution.py:224
  145.9 9.5 %gather_fusion.3 = bf16[2560,256]{1,0:T(8,128)(2,1)} fusion(bf16[8192,256]{1,0:T(8,128)(2,1)} %copy.104, s32[3072]{0:T(1024)S(1)} %pad_clamp_fusion), kind=kCustom, calls=%fused_computation.3 | custom fusion | bytes 2631680 | tf_op jit(solution)/shard_map/gather | solution.py:222
  155.4 16.5 %all-to-all-start.5 = ((bf16[32,80,256]{2,1,0:T(8,128)(2,1)}), bf16[32,80,256]{2,1,0:T(8,128)(2,1)S(1)}, u32[]{:S(2)}, u32[]{:S(2)}) async-start(bf16[32,80,256]{2,1,0:T(8,128)(2,1)} %bitcast.15), calls=%async_computation.5 | async-start | bytes 2621440 | tf_op jit(solution)/shard_map/all_to_all | solution.py:225
  172.1 0.8 gather_fusion.2
  173.2 30.5 %all-to-all-done.5 = bf16[32,80,256]{2,1,0:T(8,128)(2,1)S(1)} async-done(((bf16[32,80,256]{2,1,0:T(8,128)(2,1)}), bf16[32,80,256]{2,1,0:T(8,128)(2,1)S(1)}, u32[]{:S(2)}, u32[]{:S(2)}) %all-to-all-start.5) | async-done | bytes 1310752 | tf_op jit(solution)/shard_map/all_to_all | solution.py:225
  203.7 4.1 gather_fusion.4
  211.7 1.5 fusion.40
  213.4 1.7 scatter_custom_fusion.9
  215.1 3.6 all-to-all-start.6
  218.8 1.2 copy.101
  219.9 1.8 multiply_convert_fusion.1
  221.7 1.8 multiply_convert_fusion.2
  224.7 1.3 convolution_add_fusion.1
  226.0 9.7 %scatter_custom_fusion.10 = f32[2560,256]{1,0:T(8,128)} fusion(s32[1280]{0:T(1024)} %copy-done.37, f32[1280,256]{1,0:T(8,128)S(1)} %convolution_add_fusion.1, f32[]{:T(128)} %constant.14.clone.1), kind=kCustom, calls=%fused_computation.66 | custom fusion | bytes 2621952 | tf_op jit(solution)/shard_map/scatter | solution.py:236
  235.7 5.8 all-to-all-start.7
  243.1 1.3 add_reduce_fusion
  244.4 1.8 fusion.69
  246.2 2.2 fusion.44
  248.3 2.2 fusion.47
  250.5 51.2 %all-to-all-done.7 = f32[32,80,256]{2,1,0:T(8,128)S(1)} async-done(((f32[32,80,256]{2,1,0:T(8,128)}), f32[32,80,256]{2,1,0:T(8,128)S(1)}, u32[]{:S(2)}, u32[]{:S(2)}) %all-to-all-start.7) | async-done | bytes 2621472 | tf_op jit(solution)/shard_map/all_to_all | solution.py:246
  301.7 23.1 %scatter_custom_fusion.11 = f32[8192,256]{1,0:T(8,128)} fusion(s32[2816]{0:T(1024)} %add_reduce_fusion, f32[]{:T(128)} %constant.14.clone.1, f32[2560,256]{1,0:T(8,128)S(1)} %bitcast.149, f32[]{:T(128)} %constant.74, f32[256,256]{1,0:T(8,128)S(1)} %bitcast.155), kind=kCustom, calls=%fused_computation.53 | custom fusion | flops 1441792 | bytes 11273216 | tf_op jit(solution)/shard_map/add | solution.py:257
  324.8 9.0 %copy.103 = f32[8192,256]{0,1:T(8,128)} copy(f32[8192,256]{1,0:T(8,128)} %scatter_custom_fusion.11) | data formatting | bytes 16777216 | tf_op jit(solution)/shard_map/add | solution.py:257
  333.8 17.9 %fusion.10 = (bf16[8192,256]{0,1:T(8,128)(2,1)}, bf16[8192,256]{0,1:T(8,128)(2,1)}) fusion(f32[8192,256]{0,1:T(8,128)} %get-tuple-element.79, bf16[8192,256]{0,1:T(8,128)(2,1)} %copy.91, f32[8192,256]{0,1:T(8,128)} %copy.103, pred[8192]{0:T(1024)(128)(4,1)S(1)} %copy-done.36, f32[8192,512]{0,1:T(8,128)} %fusion.117, f32[8192,768]{0,1:T(8,128)} %fusion.113), kind=kLoop, calls=%fused_computation.36 | loop fusion | flops 35651584 | bytes 46145536 | tf_op jit(solution)/shard_map/convert_element_type | solution.py:66
  351.7 10.3 %fusion.110 = f32[256,256]{1,0:T(8,128)} fusion(bf16[8192,256]{0,1:T(8,128)(2,1)} %get-tuple-element.71, bf16[8192,256]{0,1:T(8,128)(2,1)S(1)} %copy-done.5, f32[8192,512]{0,1:T(8,128)} %fusion.117, f32[8192,768]{0,1:T(8,128)} %fusion.113), kind=kOutput, calls=%fused_computation.185 | convolution fusion | flops 1088421888 | bytes 25427968 | tf_op jit(solution)/shard_map/dot_general | solution.py:61
  362.0 9.3 %fusion.3 = bf16[8192,256]{0,1:T(8,128)(2,1)} fusion(bf16[8192,256]{0,1:T(8,128)(2,1)S(1)} %copy-done.5, bf16[256,256]{1,0:T(8,128)(2,1)S(1)} %copy-done.45, bf16[8192,256]{0,1:T(8,128)(2,1)S(1)} %copy-done.7, f32[8192,512]{0,1:T(8,128)} %fusion.117, f32[8192,768]{0,1:T(8,128)} %fusion.113), kind=kOutput, calls=%fused_computation.28 | convolution fusion | flops 1094713344 | bytes 29491200 | tf_op jit(solution)/shard_map/dot_general | solution.py:62
  371.4 9.0 %fusion.23 = f32[128,768]{1,0:T(8,128)} fusion(bf16[8192,256]{0,1:T(8,128)(2,1)S(1)} %copy-done.7, bf16[8192,256]{0,1:T(8,128)(2,1)} %fusion.3, bf16[8192,256]{0,1:T(8,128)(2,1)S(1)} %copy-done.6, f32[8192,128]{1,0:T(8,128)S(1)} %copy-done.3, f32[8192]{0:T(1024)S(1)} %copy-done.26), kind=kOutput, calls=%fused_computation.52 | convolution fusion | flops 1650458624 | bytes 17203200 | tf_op jit(solution)/shard_map/dot_general | solution.py:68
  380.5 6.7 %convolution_divide_fusion = f32[8192,128]{1,0:T(8,128)} fusion(bf16[128,768]{1,0:T(8,128)(2,1)S(1)} %copy-done.28, bf16[8192,256]{0,1:T(8,128)(2,1)S(1)} %copy-done.8, bf16[8192,256]{0,1:T(8,128)(2,1)S(1)} %copy-done.46, bf16[8192,256]{0,1:T(8,128)(2,1)S(1)} %copy-done.6, f32[8192]{0:T(1024)S(1)} %copy-done.26), kind=kOutput, calls=%fused_computation.29 | convolution fusion | flops 1649410048 | bytes 17006592 | tf_op jit(solution)/shard_map/dot_general | solution.py:70
  387.2 5.4 fusion.33
  392.6 3.3 gather_fusion.5
  396.0 1.1 fusion.58
  397.2 54.8 %all-reduce.7.cloned.1.call-done = (f32[512,128]{1,0:T(8,128)}, f32[128,768]{1,0:T(8,128)}, f32[256,512]{0,1:T(8,128)}, f32[256,256]{1,0:T(8,128)}, f32[256,256]...) async-done(((f32[512,128]{1,0:T(8,128)}, f32[128,768]{1,0:T(8,128)}, f32[256,512]{0,1:T(8,128)}, f32[256,256]{1,0:T(8,128)}, f32[256,256]{1,0:T(8,128)}, ...) | async-done | bytes 2228240 | tf_op jit(solution)/shard_map/psum | solution.py:152
  453.2 112.2 %all-reduce.5.cloned.1.call-done = (f32[512,128]{1,0:T(8,128)}, f32[128,768]{1,0:T(8,128)}, f32[256,512]{0,1:T(8,128)}, f32[256,256]{1,0:T(8,128)}, f32[256,256]...) async-done(((f32[512,128]{1,0:T(8,128)}, f32[128,768]{1,0:T(8,128)}, f32[256,512]{0,1:T(8,128)}, f32[256,256]{1,0:T(8,128)}, f32[256,256]{1,0:T(8,128)}, ...) | async-done | bytes 2228240 | tf_op jit(solution)/shard_map/psum | solution.py:153
  565.4 2.0 copy.105
  567.4 1.7 copy.171
  569.1 1.8 copy.172
  570.9 1.7 copy.173
  572.5 1.7 copy.174
  574.2 1.7 copy.175
  575.9 1.7 copy.176
  (182 shorter events, 20.8 us)
Async XLA Ops:
  7.2 32.5 %copy-start = (bf16[256,512]{1,0:T(8,128)(2,1)S(1)}, bf16[256,512]{1,0:T(8,128)(2,1)}, u32[]{:S(2)}) copy-start(bf16[256,512]{1,0:T(8,128)(2,1)} %param.28) | copy-start | bytes 786436
  15.1 48.1 %all-to-all-start = ((s32[32,2,8]{2,1,0:T(2,128)}), s32[32,2,8]{2,1,0:T(2,128)S(1)}, u32[]{:S(2)}, u32[]{:S(2)}) async-start(s32[32,2,8]{2,1,0:T(2,128)} %copy.87), calls=%async_computation | async-start | bytes 65536 | tf_op jit(solution)/shard_map/all_to_all | solution.py:192
  39.6 132.4 %copy-start.37 = (s32[1280]{0:T(1024)}, s32[1280]{0:T(1024)S(1)}, u32[]{:S(2)}) copy-start(s32[1280]{0:T(1024)S(1)} %fusion.91) | copy-start | bytes 15364
  49.9 6.5 %copy-start.42 = (s32[128,10]{0,1:T(8,128)S(1)}, s32[128,10]{0,1:T(8,128)}, u32[]{:S(2)}) copy-start(s32[128,10]{0,1:T(8,128)} %param.25) | copy-start | bytes 15364
  49.9 41.1 %copy-start.43 = (bf16[512,128]{1,0:T(8,128)(2,1)S(1)}, bf16[512,128]{1,0:T(8,128)(2,1)}, u32[]{:S(2)}) copy-start(bf16[512,128]{1,0:T(8,128)(2,1)} %param.26) | copy-start | bytes 393220
  49.9 46.8 %copy-start.27 = (bf16[128,768]{1,0:T(8,128)(2,1)S(1)}, bf16[128,768]{1,0:T(8,128)(2,1)}, u32[]{:S(2)}) copy-start(bf16[128,768]{1,0:T(8,128)(2,1)} %param.27) | copy-start | bytes 589828
  63.3 13.1 %all-to-all-start.2 = ((s32[32,2,8]{2,1,0:T(2,128)}), s32[32,2,8]{2,1,0:T(2,128)S(1)}, u32[]{:S(2)}, u32[]{:S(2)}) async-start(s32[32,2,8]{2,1,0:T(2,128)} %copy.90), calls=%async_computation.2 | async-start | bytes 65536 | tf_op jit(solution)/shard_map/all_to_all | solution.py:193
  69.2 39.4 %copy-start.40 = (f32[512]{0:T(512)}, f32[512]{0:T(512)S(1)}, u32[]{:S(2)}) copy-start(f32[512]{0:T(512)S(1)} %reshape.286) | copy-start | bytes 6148
  72.8 35.9 %copy-start.35 = (pred[8192]{0:T(1024)(128)(4,1)}, pred[8192]{0:T(1024)(128)(4,1)S(1)}, u32[]{:S(2)}) copy-start(pred[8192]{0:T(1024)(128)(4,1)S(1)} %broadcast_compare_fusion) | copy-start | bytes 24580
  72.8 35.8 %copy-start.25 = (f32[8192]{0:T(1024)}, f32[8192]{0:T(1024)S(1)}, u32[]{:S(2)}) copy-start(f32[8192]{0:T(1024)S(1)} %broadcast_maximum_fusion) | copy-start | bytes 98308
  73.4 14.4 %copy-start.38 = (s32[1024]{0:T(1024)}, s32[1024]{0:T(1024)S(1)}, u32[]{:S(2)}) copy-start(s32[1024]{0:T(1024)S(1)} %pad_clamp_fusion.4) | copy-start | bytes 12292
  76.4 11.5 %all-to-all-start.1 = ((bf16[32,2,8,128]{3,2,1,0:T(8,128)(2,1)}), bf16[32,2,8,128]{3,2,1,0:T(8,128)(2,1)S(1)}, u32[]{:S(2)}, u32[]{:S(2)}) async-start(bf16[32,2,8,128]{3,2,1,0:T(8,128)(2,1)} %pad_maximum_fusion.6), calls=%async_computation.1 | async-start | bytes 262144 | tf_op jit(solution)/shard_map/all_to_all | solution.py:204
  84.1 24.5 %copy-start.23 = (bf16[512,256]{1,0:T(8,128)(2,1)}, bf16[512,256]{1,0:T(8,128)(2,1)S(1)}, u32[]{:S(2)}) copy-start(bf16[512,256]{1,0:T(8,128)(2,1)S(1)} %gather_fusion) | copy-start | bytes 786436
  85.0 23.6 %copy-start.31 = (bf16[512,128]{1,0:T(8,128)(2,1)}, bf16[512,128]{1,0:T(8,128)(2,1)S(1)}, u32[]{:S(2)}) copy-start(bf16[512,128]{1,0:T(8,128)(2,1)S(1)} %cosine_convert_fusion) | copy-start | bytes 393220
  87.9 20.8 %copy-start.29 = (bf16[32,2,8,128]{3,2,1,0:T(8,128)(2,1)}, bf16[32,2,8,128]{3,2,1,0:T(8,128)(2,1)S(1)}, u32[]{:S(2)}) copy-start(bf16[32,2,8,128]{3,2,1,0:T(8,128)(2,1)S(1)} %all-to-all-done.1) | copy-start | bytes 393220
  87.9 51.4 %all-to-all-start.4 = ((s32[32,1,80]{2,1,0:T(1,128)}), s32[32,1,80]{2,1,0:T(1,128)S(1)}, u32[]{:S(2)}, u32[]{:S(2)}) async-start(s32[32,1,80]{2,1,0:T(1,128)} %all_to_all.31), calls=%async_computation.4 | async-start | bytes 32768 | tf_op jit(solution)/shard_map/all_to_all | solution.py:194
  91.3 17.3 %copy-start.21 = (f32[512,128]{1,0:T(8,128)}, f32[512,128]{1,0:T(8,128)S(1)}, u32[]{:S(2)}) copy-start(f32[512,128]{1,0:T(8,128)S(1)} %fusion.59) | copy-start | bytes 786436
  96.8 11.9 %copy-start.4 = (bf16[8192,256]{0,1:T(8,128)(2,1)S(1)}, bf16[8192,256]{0,1:T(8,128)(2,1)}, u32[]{:S(2)}) copy-start(bf16[8192,256]{0,1:T(8,128)(2,1)} %copy.91) | copy-start | bytes 12582916
  96.8 11.9 %copy-start.44 = (bf16[256,256]{1,0:T(8,128)(2,1)S(1)}, bf16[256,256]{1,0:T(8,128)(2,1)}, u32[]{:S(2)}) copy-start(bf16[256,256]{1,0:T(8,128)(2,1)} %param.29) | copy-start | bytes 393220
  134.9 37.0 %copy-start.16 = (bf16[128,256]{1,0:T(8,128)(2,1)S(1)}, bf16[128,256]{1,0:T(8,128)(2,1)}, u32[]{:S(2)}) copy-start(bf16[128,256]{1,0:T(8,128)(2,1)} %param.33) | copy-start | bytes 196612
  134.9 38.0 %copy-start.18 = (bf16[256,256]{1,0:T(8,128)(2,1)S(1)}, bf16[256,256]{1,0:T(8,128)(2,1)}, u32[]{:S(2)}) copy-start(bf16[256,256]{1,0:T(8,128)(2,1)} %param.30) | copy-start | bytes 393220
  139.3 16.2 %all-to-all-start.3 = ((bf16[32,8,256]{2,1,0:T(8,128)(2,1)}), bf16[32,8,256]{2,1,0:T(8,128)(2,1)S(1)}, u32[]{:S(2)}, u32[]{:S(2)}) async-start(bf16[32,8,256]{2,1,0:T(8,128)(2,1)} %bitcast.11), calls=%async_computation.3 | async-start | bytes 262144 | tf_op jit(solution)/shard_map/all_to_all | solution.py:224
  145.9 61.9 %copy-start.20 = (bf16[256,256]{1,0:T(8,128)(2,1)S(1)}, bf16[256,256]{1,0:T(8,128)(2,1)}, u32[]{:S(2)}) copy-start(bf16[256,256]{1,0:T(8,128)(2,1)} %param.32) | copy-start | bytes 393220
  155.4 53.6 %copy-start.19 = (bf16[256,256]{1,0:T(8,128)(2,1)S(1)}, bf16[256,256]{1,0:T(8,128)(2,1)}, u32[]{:S(2)}) copy-start(bf16[256,256]{1,0:T(8,128)(2,1)} %param.31) | copy-start | bytes 393220
  155.4 48.3 %all-to-all-start.5 = ((bf16[32,80,256]{2,1,0:T(8,128)(2,1)}), bf16[32,80,256]{2,1,0:T(8,128)(2,1)S(1)}, u32[]{:S(2)}, u32[]{:S(2)}) async-start(bf16[32,80,256]{2,1,0:T(8,128)(2,1)} %bitcast.15), calls=%async_computation.5 | async-start | bytes 2621440 | tf_op jit(solution)/shard_map/all_to_all | solution.py:225
  172.9 38.6 %copy-start.11 = (bf16[128,256]{1,0:T(8,128)(2,1)}, bf16[128,256]{1,0:T(8,128)(2,1)S(1)}, u32[]{:S(2)}) copy-start(bf16[128,256]{1,0:T(8,128)(2,1)S(1)} %gather_fusion.2) | copy-start | bytes 196612
  208.3 2.7 copy-start.13
  209.6 1.4 copy-start.15
  213.2 1.9 copy-start.17
  215.1 20.6 %all-to-all-start.6 = ((f32[32,8,256]{2,1,0:T(8,128)}), f32[32,8,256]{2,1,0:T(8,128)S(1)}, u32[]{:S(2)}, u32[]{:S(2)}) async-start(f32[32,8,256]{2,1,0:T(8,128)} %bitcast.25), calls=%async_computation.6 | async-start | bytes 524288 | tf_op jit(solution)/shard_map/all_to_all | solution.py:239
  219.9 21.7 %copy-start.33 = (s32[32,1,8]{2,1,0:T(1,128)S(1)}, s32[32,1,8]{2,1,0:T(1,128)}, u32[]{:S(2)}) copy-start(s32[32,1,8]{2,1,0:T(1,128)} %get-tuple-element.72) | copy-start | bytes 3076
  221.7 3.0 copy-start.10
  223.5 0.8 copy-start.9
  235.7 66.0 %all-to-all-start.7 = ((f32[32,80,256]{2,1,0:T(8,128)}), f32[32,80,256]{2,1,0:T(8,128)S(1)}, u32[]{:S(2)}, u32[]{:S(2)}) async-start(f32[32,80,256]{2,1,0:T(8,128)} %bitcast.29), calls=%async_computation.7 | async-start | bytes 5242880 | tf_op jit(solution)/shard_map/all_to_all | solution.py:246
  241.6 210.3 %all-reduce.7.cloned.1.call-start = ((), (), s32[]{:S(2)}) async-start(), calls=%async_computation.9 | async-start | bytes 4456448 | tf_op jit(solution)/shard_map/psum | solution.py:152
  324.8 9.0 %copy-start.36 = (pred[8192]{0:T(1024)(128)(4,1)S(1)}, pred[8192]{0:T(1024)(128)(4,1)}, u32[]{:S(2)}) copy-start(pred[8192]{0:T(1024)(128)(4,1)} %copy-done.35) | copy-start | bytes 24580
  333.8 17.9 %copy-start.5 = (bf16[8192,256]{0,1:T(8,128)(2,1)S(1)}, bf16[8192,256]{0,1:T(8,128)(2,1)}, u32[]{:S(2)}) copy-start(bf16[8192,256]{0,1:T(8,128)(2,1)} %copy.91) | copy-start | bytes 12582916
  351.7 10.3 %copy-start.7 = (bf16[8192,256]{0,1:T(8,128)(2,1)S(1)}, bf16[8192,256]{0,1:T(8,128)(2,1)}, u32[]{:S(2)}) copy-start(bf16[8192,256]{0,1:T(8,128)(2,1)} %get-tuple-element.71) | copy-start | bytes 12582916
  351.7 10.3 %copy-start.45 = (bf16[256,256]{1,0:T(8,128)(2,1)S(1)}, bf16[256,256]{1,0:T(8,128)(2,1)}, u32[]{:S(2)}) copy-start(bf16[256,256]{1,0:T(8,128)(2,1)} %param.29) | copy-start | bytes 393220
  362.0 9.3 %copy-start.3 = (f32[8192,128]{1,0:T(8,128)S(1)}, f32[8192,128]{1,0:T(8,128)}, u32[]{:S(2)}) copy-start(f32[8192,128]{1,0:T(8,128)} %scatter_custom_fusion.7) | copy-start | bytes 12582916
  362.0 9.4 %copy-start.6 = (bf16[8192,256]{0,1:T(8,128)(2,1)S(1)}, bf16[8192,256]{0,1:T(8,128)(2,1)}, u32[]{:S(2)}) copy-start(bf16[8192,256]{0,1:T(8,128)(2,1)} %get-tuple-element.70) | copy-start | bytes 12582916
  362.0 9.4 %copy-start.26 = (f32[8192]{0:T(1024)S(1)}, f32[8192]{0:T(1024)}, u32[]{:S(2)}) copy-start(f32[8192]{0:T(1024)} %copy-done.25) | copy-start | bytes 98308
  371.4 9.0 %copy-start.8 = (bf16[8192,256]{0,1:T(8,128)(2,1)S(1)}, bf16[8192,256]{0,1:T(8,128)(2,1)}, u32[]{:S(2)}) copy-start(bf16[8192,256]{0,1:T(8,128)(2,1)} %get-tuple-element.71) | copy-start | bytes 12582916
  371.4 9.0 %copy-start.28 = (bf16[128,768]{1,0:T(8,128)(2,1)S(1)}, bf16[128,768]{1,0:T(8,128)(2,1)}, u32[]{:S(2)}) copy-start(bf16[128,768]{1,0:T(8,128)(2,1)} %param.27) | copy-start | bytes 589828
  371.4 9.0 %copy-start.46 = (bf16[8192,256]{0,1:T(8,128)(2,1)S(1)}, bf16[8192,256]{0,1:T(8,128)(2,1)}, u32[]{:S(2)}) copy-start(bf16[8192,256]{0,1:T(8,128)(2,1)} %fusion.3) | copy-start | bytes 12582916
  380.5 6.7 %copy-start.2 = (bf16[8192,256]{1,0:T(8,128)(2,1)S(1)}, bf16[8192,256]{1,0:T(8,128)(2,1)}, u32[]{:S(2)}) copy-start(bf16[8192,256]{1,0:T(8,128)(2,1)} %param.17) | copy-start | bytes 12582916
  387.1 5.5 copy-start.39
  387.1 8.8 %copy-start.22 = (f32[512,128]{1,0:T(8,128)S(1)}, f32[512,128]{1,0:T(8,128)}, u32[]{:S(2)}) copy-start(f32[512,128]{1,0:T(8,128)} %copy-done.21) | copy-start | bytes 786436
  387.1 8.8 %copy-start.24 = (bf16[512,256]{1,0:T(8,128)(2,1)S(1)}, bf16[512,256]{1,0:T(8,128)(2,1)}, u32[]{:S(2)}) copy-start(bf16[512,256]{1,0:T(8,128)(2,1)} %copy-done.23) | copy-start | bytes 786436
  387.2 8.8 %copy-start.30 = (bf16[32,2,8,128]{3,2,1,0:T(8,128)(2,1)S(1)}, bf16[32,2,8,128]{3,2,1,0:T(8,128)(2,1)}, u32[]{:S(2)}) copy-start(bf16[32,2,8,128]{3,2,1,0:T(8,128)(2,1)} %copy-done.29) | copy-start | bytes 393220
  387.2 8.8 %copy-start.32 = (bf16[512,128]{1,0:T(8,128)(2,1)S(1)}, bf16[512,128]{1,0:T(8,128)(2,1)}, u32[]{:S(2)}) copy-start(bf16[512,128]{1,0:T(8,128)(2,1)} %copy-done.31) | copy-start | bytes 393220
  387.2 8.8 %copy-start.41 = (f32[512]{0:T(512)S(1)}, f32[512]{0:T(512)}, u32[]{:S(2)}) copy-start(f32[512]{0:T(512)} %copy-done.40) | copy-start | bytes 6148
  387.2 190.4 %copy-start.1 = (bf16[256,512]{1,0:T(8,128)(2,1)S(1)}, bf16[256,512]{1,0:T(8,128)(2,1)}, u32[]{:S(2)}) copy-start(bf16[256,512]{1,0:T(8,128)(2,1)} %param.28) | copy-start | bytes 786436
  392.6 59.3 %copy-start.34 = (bf16[128,2,10]{0,1,2:T(2,128)(2,1)S(1)}, bf16[128,2,10]{0,1,2:T(2,128)(2,1)}, u32[]{:S(2)}) copy-start(bf16[128,2,10]{0,1,2:T(2,128)(2,1)} %get-tuple-element.77) | copy-start | bytes 15364
  392.6 59.5 %copy-start.14 = (bf16[128,10,2,128]{3,2,1,0:T(2,128)(2,1)S(1)}, bf16[128,10,2,128]{3,2,1,0:T(2,128)(2,1)}, u32[]{:S(2)}) copy-start(bf16[128,10,2,128]{3,2,1,0:T(2,128)(2,1)} %copy-done.13) | copy-start | bytes 1966084
  392.6 59.9 %copy-start.12 = (bf16[128,256]{1,0:T(8,128)(2,1)S(1)}, bf16[128,256]{1,0:T(8,128)(2,1)}, u32[]{:S(2)}) copy-start(bf16[128,256]{1,0:T(8,128)(2,1)} %copy-done.11) | copy-start | bytes 196612
  397.1 168.3 %all-reduce.5.cloned.1.call-start = ((), (), s32[]{:S(2)}) async-start(), calls=%async_computation.8 | async-start | bytes 4456448 | tf_op jit(solution)/shard_map/psum | solution.py:153
Sparse Core Ops, SparseCore 0:
  397.2 54.6 all-reduce.6
  456.5 108.8 all-reduce.4
